TPU v7x, 256 devices: a whole 4x4x8 slice. The times are simulated.
256 devices in a mesh: seq: 32 (over y, x, core), tp: 8 (over z).
Axes of the slice: x: 4, y: 4, z: 8, core: 2. Of those that a mesh axis runs over, the one named last changes fastest.
Arguments:
- tokens: bfloat16 [8192, 4096], P('seq', 'tp'), may hold values from -11 to 11
- grad_out: bfloat16 [8192, 4096], P('seq', 'tp'), may hold values from -1.5 to 1.5
- in_weight: bfloat16 [4096, 4096], P('seq', 'tp'), may hold values from -0.09880682 to 0.09880682
- in_scale: float32 [4096], P('tp'), may hold values from 0.0008238636 to 0.010511364
- out_weight: bfloat16 [4096, 4096], P('seq', 'tp'), may hold values from -0.053943182 to 0.053943182
- out_scale: float32 [4096], replicated, may hold values from 0.00139204545 to 0.0057386364
- state_in: bfloat16 [8192, 128], P('seq'), may hold values from -0.0625 to 0.0625
- state_out: bfloat16 [8192, 128], P('seq'), may hold values from -6 to 6
- log_decay: float32 [8192, 64], P('seq', 'tp'), may hold values from -1.6 to 0
Outputs:
- grad_tokens: bfloat16 [8192, 4096], P('seq', 'tp')
- grad_in_weight: float32 [4096, 4096], P('seq', 'tp')
- grad_in_scale: float32 [4096], P('tp')
- grad_out_weight: float32 [4096, 4096], P('seq', 'tp')
- grad_out_scale: float32 [4096], P('seq')
All inputs are finite; a program needn't handle non-finite values.
Results may differ from a plain program's by a relative error of at most 0.027.
Values may be sent and summed in bfloat16 or wider, within the bound.
No kernel may reach another device: no remote copies, remote signals or barrier semaphores. Data moves between devices by JAX's collectives and lax.ppermute only.
A program may use at most 128 MiB of HBM per device.

v0:
```python
import jax
import jax.numpy as jnp
from jax import lax
from jax.sharding import PartitionSpec as P

D = 4096
HEADS = 64
HEAD_DIM = 64
STRETCH = 256
QMAX = 7
precise = lax.Precision.HIGHEST


def prefix(array, axis, join, neutral, backward):
    count = lax.axis_size(axis)
    place = lax.axis_index(axis)
    ahead = count - 1 - place if backward else place
    gathered = jax.tree.map(
        lambda a, kind: lax.all_gather(a.astype(kind), axis), array, (jnp.bfloat16, jnp.bfloat16)
    )
    state = jax.tree.map(lambda a, e: jnp.zeros_like(a) + jnp.asarray(e, a.dtype), array, neutral)

    def one(turn, state):
        source = count - 1 - turn if backward else turn
        return join(
            state,
            jax.tree.map(
                lambda a, own: lax.dynamic_index_in_dim(a, source, 0, False).astype(own.dtype),
                gathered,
                array,
            ),
        )

    return lax.fori_loop(0, ahead, one, state)


def quantize(weight, channel_scale):
    ratios = weight.astype(jnp.float32) / channel_scale
    clipped = jnp.clip(ratios, -QMAX, QMAX)
    levels = jnp.floor(clipped + 0.5)
    inside = jnp.abs(ratios) <= QMAX
    slopes = jnp.where(inside, levels - ratios, levels)
    return (levels, slopes, inside.astype(jnp.float32))


def stretch_terms(decay_logs, inputs_f, outputs_f):
    cumul = jnp.cumsum(decay_logs, axis=0)
    ending = cumul[-1]
    spread = cumul[:, None, :] - cumul[None, :, :]
    length = decay_logs.shape[0]
    causal = jnp.arange(length)[:, None] >= jnp.arange(length)[None, :]
    mixing = jnp.exp(jnp.where(causal[:, :, None], spread, -jnp.inf))
    intersection = jnp.dot(outputs_f, inputs_f.T, precision=precise)
    return (cumul, ending, mixing * intersection[:, :, None])


def forward_step(carried, pieces):
    values, cumul, ending, weights, inputs_f, outputs_f = pieces
    inner = jnp.einsum("sth,thp->shp", weights, values, precision=precise)
    outer = jnp.exp(cumul)[:, :, None] * jnp.einsum(
        "sn,hnp->shp", outputs_f, carried, precision=precise
    )
    fresh = jnp.einsum(
        "th,tn,thp->hnp", jnp.exp(ending[None, :] - cumul), inputs_f, values, precision=precise
    )
    return (jnp.exp(ending)[:, None, None] * carried + fresh, inner + outer)


def backward_step(carried, pieces):
    grads, cumul, ending, weights, inputs_f, outputs_f = pieces
    inner = jnp.einsum("sth,shp->thp", weights, grads, precision=precise)
    outer = jnp.exp(ending[None, :] - cumul)[:, :, None] * jnp.einsum(
        "tn,hnp->thp", inputs_f, carried, precision=precise
    )
    fresh = jnp.einsum("sh,sn,shp->hnp", jnp.exp(cumul), outputs_f, grads, precision=precise)
    return (jnp.exp(ending)[:, None, None] * carried + fresh, inner + outer)


def join_forward(earlier, later):
    return (earlier[0] * later[0], later[0][:, None, None] * earlier[1] + later[1])


def join_backward(earlier, later):
    return (earlier[0] * later[0], later[1] + later[0][:, None, None] * earlier[1])


def per_device(
    tokens, grad_out, in_weight, in_scale, out_weight, out_scale, state_in, state_out, log_decay
):
    local_rows = tokens.shape[0]
    heads_here = log_decay.shape[1]
    width_here = in_scale.shape[0]
    head_size = width_here // heads_here
    state_size = state_in.shape[1]
    weight_rows = in_weight.shape[0]
    blocks = local_rows // STRETCH
    row_start = lax.axis_index("seq") * weight_rows
    out_scale_rows = lax.dynamic_slice_in_dim(out_scale, row_start, weight_rows)
    in_levels, in_slopes, in_inside = quantize(in_weight, in_scale[None, :])
    out_levels, out_slopes, out_inside = quantize(out_weight, out_scale_rows[:, None])
    in_codes = lax.all_gather(in_levels.astype(jnp.bfloat16), "seq", axis=0, tiled=True)
    out_codes = lax.all_gather(out_levels.astype(jnp.bfloat16), "seq", axis=0, tiled=True)
    features = lax.all_gather(tokens, "tp", axis=1, tiled=True)
    cotangent = lax.all_gather(grad_out, "tp", axis=1, tiled=True)
    projected = jnp.dot(features, in_codes, preferred_element_type=jnp.float32) * in_scale[None, :]
    scaled_grad = (cotangent.astype(jnp.float32) * out_scale[None, :]).astype(jnp.bfloat16)
    grad_mixed = jnp.dot(scaled_grad, out_codes, preferred_element_type=jnp.float32)
    inputs_full = state_in.astype(jnp.float32)
    outputs_full = state_out.astype(jnp.float32)
    decay_blocks = log_decay.reshape(blocks, STRETCH, heads_here)
    input_blocks = inputs_full.reshape(blocks, STRETCH, state_size)
    output_blocks = outputs_full.reshape(blocks, STRETCH, state_size)
    cumul, ending, weights = jax.vmap(stretch_terms)(decay_blocks, input_blocks, output_blocks)
    value_blocks = projected.reshape(blocks, STRETCH, heads_here, head_size)
    grad_blocks = grad_mixed.reshape(blocks, STRETCH, heads_here, head_size)
    empty = jnp.zeros((heads_here, state_size, head_size), jnp.float32)
    local_state, mixed_local = lax.scan(
        forward_step, empty, (value_blocks, cumul, ending, weights, input_blocks, output_blocks)
    )
    local_grad_state, grad_local = lax.scan(
        backward_step,
        empty,
        (grad_blocks, cumul, ending, weights, input_blocks, output_blocks),
        reverse=True,
    )
    running = jnp.cumsum(log_decay, axis=0)
    device_total = running[-1]
    device_decay = jnp.exp(device_total)
    identity = (jnp.ones_like(device_decay), empty)
    entering = prefix((device_decay, local_state), "seq", join_forward, identity, False)[1]
    leaving = prefix((device_decay, local_grad_state), "seq", join_backward, identity, True)[1]
    mixed = mixed_local.reshape(local_rows, heads_here, head_size) + jnp.exp(running)[
        :, :, None
    ] * jnp.einsum("tn,hnp->thp", outputs_full, entering, precision=precise)
    grad_values = grad_local.reshape(local_rows, heads_here, head_size) + jnp.exp(
        device_total[None, :] - running
    )[:, :, None] * jnp.einsum("tn,hnp->thp", inputs_full, leaving, precision=precise)
    mixed = mixed.reshape(local_rows, width_here)
    grad_values = grad_values.reshape(local_rows, width_here)
    mixed_b = mixed.astype(jnp.bfloat16)
    grad_b = grad_values.astype(jnp.bfloat16)
    grad_scaled = (grad_values * in_scale[None, :]).astype(jnp.bfloat16)
    piece = features
    in_total = lax.psum_scatter(
        jnp.einsum("td,tc->dc", piece, grad_b, preferred_element_type=jnp.float32).astype(
            jnp.bfloat16
        ),
        "seq",
        scatter_dimension=0,
        tiled=True,
    ).astype(jnp.float32)
    piece = cotangent
    out_total = lax.psum_scatter(
        jnp.einsum("td,tc->dc", piece, mixed_b, preferred_element_type=jnp.float32).astype(
            jnp.bfloat16
        ),
        "seq",
        scatter_dimension=0,
        tiled=True,
    ).astype(jnp.float32)
    partial_tokens = jnp.einsum(
        "tc,dc->td", grad_scaled, in_codes, preferred_element_type=jnp.float32
    )
    grad_tokens = lax.psum_scatter(
        partial_tokens.astype(jnp.bfloat16), "tp", scatter_dimension=1, tiled=True
    )
    in_part = jnp.sum(in_total * in_slopes, axis=0)
    out_part = jnp.sum(out_total * out_slopes, axis=1)
    in_sum = lax.psum(in_part, "seq")
    out_sum = lax.psum(out_part, "tp")
    grad_in_scale = in_sum / jnp.sqrt(jnp.float32(D * QMAX))
    grad_out_scale = out_sum / jnp.sqrt(jnp.float32(HEADS * HEAD_DIM * QMAX))
    return (
        grad_tokens,
        in_total * in_inside,
        grad_in_scale,
        out_total * out_inside,
        grad_out_scale,
    )


def solution(mesh):
    placed = (
        P("seq", "tp"),
        P("seq", "tp"),
        P("seq", "tp"),
        P("tp"),
        P("seq", "tp"),
        P(),
        P("seq", None),
        P("seq", None),
        P("seq", "tp"),
    )
    return jax.shard_map(
        per_device,
        mesh=mesh,
        in_specs=placed,
        out_specs=(P("seq", "tp"), P("seq", "tp"), P("tp"), P("seq", "tp"), P("seq")),
        check_vma=False,
    )
```

profile of v0, /device:TPU:6, one launch (start us, length us, event | category | flops | bytes accessed | tf_op | source)
XLA Modules:
  0.0 612.6 jit_solution(15400213899961906926)
XLA Ops:
  10.5 1.3 reduce-window.14
  12.4 41.5 %all-gather.10.cloned.1.call-done = bf16[256,4096]{1,0:T(8,128)(2,1)} async-done(((bf16[256,512]{1,0:T(8,128)(2,1)}), bf16[256,4096]{1,0:T(8,128)(2,1)}) %all-gather.10.cloned.1.call-update) | async-done | bytes 2097168 | tf_op jit(solution)/shard_map/all_gather | solution.py:104
  53.9 55.4 %all-gather.12.cloned.1.call-done = bf16[4096,512]{0,1:T(8,128)(2,1)} async-done(((bf16[128,512]{0,1:T(8,128)(2,1)}), bf16[4096,512]{0,1:T(8,128)(2,1)}) %all-gather.12.cloned.1.call-update) | async-done | bytes 4194320 | tf_op jit(solution)/shard_map/all_gather | solution.py:102
  109.3 4.1 fusion.2
  116.2 18.9 %all-gather.2 = bf16[32,1,8]{2,1,0:T(2,128)(2,1)S(1)} all-gather(bf16[1,1,8]{2,1,0:T(2,128)(2,1)S(1)} %bitcast.154), channel_id=1, replica_groups=mesh['seq'=32,'tp'=8] {'seq'}, dimensions={0}, use_global_device_ids=true | all-gather | bytes 528 | tf_op jit(solution)/shard_map/all_gather | solution.py:19
  135.6 1.8 fusion.6
  137.5 28.1 %all-gather.18.cloned.1.call-done = bf16[256,128,64]{1,2,0:T(8,128)(2,1)} async-done(((bf16[8,128,64]{1,2,0:T(8,128)(2,1)}), bf16[256,128,64]{1,2,0:T(8,128)(2,1)}) %all-gather.18.cloned.1.call-update) | async-done | bytes 4194320 | tf_op jit(solution)/shard_map/all_gather | solution.py:19
  165.6 32.6 %while.16 = (s32[]{:T(128)}, f32[8,128,64]{2,1,0:T(8,128)S(1)}, s32[]{:T(128)}, bf16[32,8,128,64]{2,3,1,0:T(8,128)(2,1)}, bf16[32,8]{1,0:T(8,128)(2,1)S(1)}, /*index=5*/s32[]{:T(128)}, s32[]{:T(128)}, s32[]{:T(128)}, s32[]{:T(128)}) while((s32[]{:T(128)}, f32[8,128,64]{2,1,0:T(8,128)S(1)}, s32[]{:T(128)}, bf16[32,8,128,64]{2,3,1,0:T(8,128)(2,1)}, ...), condition=%wide.region_5.6_spmd, body=%wide.region_4.5_spmd.sunk | while | flops 196622 | bytes 1179883 | solution.py:34
  199.3 8.6 %all-gather.16.cloned.1.call-done = bf16[256,4096]{1,0:T(8,128)(2,1)} async-done(((bf16[256,512]{1,0:T(8,128)(2,1)}), bf16[256,4096]{1,0:T(8,128)(2,1)}) %all-gather.16.cloned.1.call-update) | async-done | bytes 2097168 | tf_op jit(solution)/shard_map/all_gather | solution.py:103
  207.9 4.8 fusion
  212.7 6.5 %copy.81 = bf16[4096,512]{1,0:T(8,128)(2,1)} copy(bf16[4096,512]{0,1:T(8,128)(2,1)} %fusion) | data formatting | bytes 8388608
  220.2 87.2 %reduce-scatter.10.cloned.1.call-done = bf16[128,512]{1,0:T(8,128)(2,1)} async-done(((bf16[4096,512]{1,0:T(8,128)(2,1)}), bf16[128,512]{1,0:T(8,128)(2,1)}) %reduce-scatter.10.cloned.1.call-update) | async-done | bytes 131088
  309.3 54.8 %all-gather.14.cloned.1.call-done = bf16[4096,512]{0,1:T(8,128)(2,1)} async-done(((bf16[128,512]{0,1:T(8,128)(2,1)}), bf16[4096,512]{0,1:T(8,128)(2,1)}) %all-gather.14.cloned.1.call-update) | async-done | bytes 4194320 | tf_op jit(solution)/shard_map/all_gather | solution.py:101
  364.1 3.5 convolution_multiply_fusion
  369.6 3.5 fusion.7
  373.0 47.4 %all-gather.20.cloned.1.call-done = bf16[256,128,64]{1,2,0:T(8,128)(2,1)} async-done(((bf16[8,128,64]{1,2,0:T(8,128)(2,1)}), bf16[256,128,64]{1,2,0:T(8,128)(2,1)}) %all-gather.20.cloned.1.call-update) | async-done | bytes 4194320 | tf_op jit(solution)/shard_map/all_gather | solution.py:19
  420.5 8.0 %while.17 = (s32[]{:T(128)}, f32[8,128,64]{2,1,0:T(8,128)S(1)}, s32[]{:T(128)}, bf16[32,8]{1,0:T(8,128)(2,1)S(1)}, bf16[32,8,128,64]{2,3,1,0:T(8,128)(2,1)}, /*index=5*/s32[]{:T(128)}, s32[]{:T(128)}, s32[]{:T(128)}) while((s32[]{:T(128)}, f32[8,128,64]{2,1,0:T(8,128)S(1)}, s32[]{:T(128)}, bf16[32,8]{1,0:T(8,128)(2,1)S(1)}, ...), condition=%wide.region_11.12_spmd, body=%wide.region_10.11_spmd.sunk | while | flops 196621 | bytes 1179863 | solution.py:34
  430.1 3.2 fusion.1
  433.4 6.5 %copy.83 = bf16[4096,512]{1,0:T(8,128)(2,1)} copy(bf16[4096,512]{0,1:T(8,128)(2,1)} %fusion.1) | data formatting | bytes 8388608
  440.1 4.9 convolution_convert_fusion.2
  445.8 83.4 %psum.14 = f32[512]{0:T(512)S(1)} all-reduce(f32[512]{0:T(512)S(1)} %get-tuple-element.273), channel_id=1, replica_groups=mesh['seq'=32,'tp'=8] {'seq'}, use_global_device_ids=true, to_apply=%region_9.10 | all-reduce | flops 512 | bytes 4096 | tf_op jit(solution)/shard_map/psum | solution.py:169
  529.8 31.0 %reduce-scatter.12.cloned.1.call-done = bf16[128,512]{1,0:T(8,128)(2,1)} async-done(((bf16[4096,512]{1,0:T(8,128)(2,1)}), bf16[128,512]{1,0:T(8,128)(2,1)}) %reduce-scatter.12.cloned.1.call-update) | async-done | bytes 131088
  562.8 17.4 %psum.15 = f32[128]{0:T(128)S(1)} all-reduce(f32[128]{0:T(128)S(1)} %get-tuple-element.275), channel_id=1, replica_groups=mesh['seq'=32,'tp'=8] {'tp'}, use_global_device_ids=true, to_apply=%region_14.15 | all-reduce | flops 128 | bytes 1024 | tf_op jit(solution)/shard_map/psum | solution.py:170
  580.7 25.3 %reduce-scatter.8.cloned.1.call-done = bf16[256,512]{1,0:T(8,128)(2,1)} async-done(((bf16[256,4096]{1,0:T(8,128)(2,1)}), bf16[256,512]{1,0:T(8,128)(2,1)}) %reduce-scatter.8.cloned.1.call-update) | async-done | bytes 262160 | tf_op jit(solution)/shard_map/reduce_scatter | solution.py:164
  (203 shorter events, 58.0 us)
Async XLA Ops:
  7.2 128.3 %copy-start = (bf16[256,128]{1,0:T(8,128)(2,1)S(1)}, bf16[256,128]{1,0:T(8,128)(2,1)}, u32[]{:S(2)}) copy-start(bf16[256,128]{1,0:T(8,128)(2,1)} %param.19) | copy-start | bytes 196612
  7.2 46.7 %all-gather.10.cloned.1.call-start = ((), (), s32[]{:S(2)}) async-start(), calls=%async_computation.3 | async-start | bytes 2359296 | tf_op jit(solution)/shard_map/all_gather | solution.py:104
  7.9 101.4 %all-gather.12.cloned.1.call-start = ((), (), s32[]{:S(2)}) async-start(), calls=%async_computation.4 | async-start | bytes 4325376 | tf_op jit(solution)/shard_map/all_gather | solution.py:102
  10.5 155.0 %all-gather.18.cloned.1.call-start = ((), (), s32[]{:S(2)}) async-start(), calls=%async_computation.8 | async-start | bytes 4325376 | tf_op jit(solution)/shard_map/all_gather | solution.py:19
  12.4 101.1 %copy-start.3 = (bf16[256,128]{1,0:T(8,128)(2,1)S(1)}, bf16[256,128]{1,0:T(8,128)(2,1)}, u32[]{:S(2)}) copy-start(bf16[256,128]{1,0:T(8,128)(2,1)} %param.20) | copy-start | bytes 196612
  12.4 102.8 %copy-start.8 = (f32[256,8]{0,1:T(8,128)S(1)}, f32[256,8]{0,1:T(8,128)}, u32[]{:S(2)}) copy-start(f32[256,8]{0,1:T(8,128)} %param.21) | copy-start | bytes 24580
  114.5 93.4 %all-gather.16.cloned.1.call-start = ((), (), s32[]{:S(2)}) async-start(), calls=%async_computation.7 | async-start | bytes 2359296 | tf_op jit(solution)/shard_map/all_gather | solution.py:103
  115.1 192.3 %reduce-scatter.10.cloned.1.call-start = ((), (), s32[]{:S(2)}) async-start(), calls=%async_computation.10 | async-start | bytes 4325376
  135.6 30.0 %copy-start.5 = (f32[256,256]{1,0:T(8,128)}, f32[256,256]{1,0:T(8,128)S(1)}, u32[]{:S(2)}) copy-start(f32[256,256]{1,0:T(8,128)S(1)} %fusion.57) | copy-start | bytes 786436
  219.2 0.9 copy-start.7
  219.2 89.2 %copy-start.9 = (f32[512]{0:T(512)S(1)}, f32[512]{0:T(512)}, u32[]{:S(2)}) copy-start(f32[512]{0:T(512)} %param.16) | copy-start | bytes 6148
  219.2 145.0 %copy-start.2 = (bf16[256,4096]{1,0:T(8,128)(2,1)S(1)}, bf16[256,4096]{1,0:T(8,128)(2,1)}, u32[]{:S(2)}) copy-start(bf16[256,4096]{1,0:T(8,128)(2,1)} %all-gather.16.cloned.1.call-done) | copy-start | bytes 6291460
  219.2 145.0 %all-gather.14.cloned.1.call-start = ((), (), s32[]{:S(2)}) async-start(), calls=%async_computation.5 | async-start | bytes 4325376 | tf_op jit(solution)/shard_map/all_gather | solution.py:101
  309.3 60.3 %copy-start.6 = (f32[256,256]{1,0:T(8,128)S(1)}, f32[256,256]{1,0:T(8,128)}, u32[]{:S(2)}) copy-start(f32[256,256]{1,0:T(8,128)} %copy-done.5) | copy-start | bytes 786436
  309.3 111.2 %all-gather.20.cloned.1.call-start = ((), (), s32[]{:S(2)}) async-start(), calls=%async_computation.9 | async-start | bytes 4325376 | tf_op jit(solution)/shard_map/all_gather | solution.py:19
  367.6 0.8 copy-start.4
  369.5 191.3 %reduce-scatter.12.cloned.1.call-start = ((), (), s32[]{:S(2)}) async-start(), calls=%async_computation.11 | async-start | bytes 4325376
  428.5 1.6 copy-start.1
  439.9 166.1 %reduce-scatter.8.cloned.1.call-start = ((), (), s32[]{:S(2)}) async-start(), calls=%async_computation.6 | async-start | bytes 2359296 | tf_op jit(solution)/shard_map/reduce_scatter | solution.py:164
Sparse Core Ops, SparseCore 0:
  9.8 44.0 all-gather.9
  56.9 52.3 all-gather.11
  114.6 50.8 all-gather.17
  167.2 40.6 all-gather.15
  219.3 88.0 reduce-scatter.9
  310.6 53.5 all-gather.13
  369.6 50.7 all-gather.19
  440.0 120.7 reduce-scatter.11
  563.9 42.0 reduce-scatter.7
where the time goes:
time: 614 us; the launch traced here: 613 us
  waiting for transfers between devices  381 us (62%)
  blocking collectives  120 us (20%)
  local copies, waits for them, and re-layouts  55.6 us (9%)
  matrix products  30.2 us (5%)
  between operations  14.1 us (2%)
  other arithmetic  10.6 us (2%)
    unnamed x11, waiting for transfers between devices  119 us
    psum x1, blocking collectives, per_device(): in_sum = lax.psum(in_part, 'seq')  83.4 us
    all_gather x2, waiting for transfers between devices, prefix(): lax.all_gather(a.astype(kind), axis)  75.5 us
    all_gather x1, waiting for transfers between devices, per_device(): lax.all_gather(out_levels.astype(jnp.bfloat16), 'seq', axis=0, tiled=True)  55.4 us
    all_gather x1, waiting for transfers between devices, per_device(): lax.all_gather(in_levels.astype(jnp.bfloat16), 'seq', axis=0, tiled=True)  54.8 us
    all_gather x1, waiting for transfers between devices, per_device(): cotangent = lax.all_gather(grad_out, 'tp', axis=1, tiled=True)  41.5 us
    dynamic_slice x62, local copies, waits for them, and re-layouts, one(): lax.dynamic_index_in_dim(a, source, 0, False).astype(own.dtype)  34 us
    reduce_scatter x1, waiting for transfers between devices, per_device(): lax.psum_scatter(partial_tokens.astype(jnp.bfloat16), 'tp', scatter_dimen...  25.3 us
  transfers between devices with their start and end apart: 9, of which 9 were waited for; matrix products, arithmetic and copies ran while one was open for 9% of the time, Pallas kernels for 0%

commit v1 on v0

--- a/solution.py
+++ b/solution.py
@@ -101,7 +101,12 @@
     in_codes = lax.all_gather(in_levels.astype(jnp.bfloat16), "seq", axis=0, tiled=True)
     out_codes = lax.all_gather(out_levels.astype(jnp.bfloat16), "seq", axis=0, tiled=True)
     features = lax.all_gather(tokens, "tp", axis=1, tiled=True)
-    cotangent = lax.all_gather(grad_out, "tp", axis=1, tiled=True)
+    ring = [grad_out]
+    for hop in range(7):
+        ring.append(lax.ppermute(ring[-1], "tp", [(dev, (dev + 1) % 8) for dev in range(8)]))
+    cotangent = jnp.roll(
+        jnp.concatenate(ring[::-1], axis=1), (lax.axis_index("tp") + 1) * ring[0].shape[1], axis=1
+    )
     projected = jnp.dot(features, in_codes, preferred_element_type=jnp.float32) * in_scale[None, :]
     scaled_grad = (cotangent.astype(jnp.float32) * out_scale[None, :]).astype(jnp.bfloat16)
     grad_mixed = jnp.dot(scaled_grad, out_codes, preferred_element_type=jnp.float32)

time: 614 us -> 585 us (0.953)
  waiting for transfers between devices: 381 us -> 339 us
    ppermute x0 -> x7, waiting for transfers between devices: none -> 58.5 us  [per_device(): lax.ppermute(ring[-1], 'tp', [(dev, (dev + 1) % 8) for dev in range(8)])]
    all_gather x1, waiting for transfers between devices: 55.4 us -> 0.01 us  [per_device(): lax.all_gather(out_levels.astype(jnp.bfloat16), 'seq', axis=0, tiled=True)]
    all_gather x1 -> x0, waiting for transfers between devices: 41.5 us -> none  [per_device(): cotangent = lax.all_gather(grad_out, 'tp', axis=1, tiled=True)]
    unnamed x28 -> x44, local copies, waits for them, and re-layouts: 20.1 us -> 25.1 us
    unnamed x11 -> x10, waiting for transfers between devices: 119 us -> 119 us
  transfers between devices with their start and end apart: 9 -> 15, of which waited for: 9 -> 14; matrix products, arithmetic and copies ran while one was open for 9% -> 11% of each run, Pallas kernels for 0% -> 0%
where the time goes in v1:
time: 585 us; the launch traced here: 583 us
  waiting for transfers between devices  339 us (58%)
  blocking collectives  122 us (21%)
  local copies, waits for them, and re-layouts  61.3 us (10%)
  matrix products  31.9 us (5%)
  between operations  14.4 us (2%)
  other arithmetic  10.6 us (2%)
    unnamed x10, waiting for transfers between devices  119 us
    psum x1, blocking collectives, per_device(): in_sum = lax.psum(in_part, 'seq')  83.4 us
    all_gather x2, waiting for transfers between devices, prefix(): lax.all_gather(a.astype(kind), axis)  73.5 us
    ppermute x7, waiting for transfers between devices, per_device(): lax.ppermute(ring[-1], 'tp', [(dev, (dev + 1) % 8) for dev in range(8)])  58.5 us
    all_gather x1, waiting for transfers between devices, per_device(): lax.all_gather(in_levels.astype(jnp.bfloat16), 'seq', axis=0, tiled=True)  54.8 us
    dynamic_slice x62, local copies, waits for them, and re-layouts, one(): lax.dynamic_index_in_dim(a, source, 0, False).astype(own.dtype)  34 us
    reduce_scatter x1, waiting for transfers between devices, per_device(): lax.psum_scatter(partial_tokens.astype(jnp.bfloat16), 'tp', scatter_dimen...  25.1 us
    unnamed x44, local copies, waits for them, and re-layouts  25.1 us
  transfers between devices with their start and end apart: 15, of which 14 were waited for; matrix products, arithmetic and copies ran while one was open for 11% of the time, Pallas kernels for 0%

profile of v1, /device:TPU:6, one launch (start us, length us, event | category | flops | bytes accessed | tf_op | source)
XLA Modules:
  0.0 583.2 jit_solution(7646458932287434820)
XLA Ops:
  11.9 10.5 %collective-permute-done = bf16[256,512]{1,0:T(8,128)(2,1)S(1)} collective-permute-done((bf16[256,512]{1,0:T(8,128)(2,1)}, bf16[256,512]{1,0:T(8,128)(2,1)S(1)}, u32[]{:S(2)}, u32[]{:S(2)}) %collective-permute-start) | collective-permute-done | bytes 262176 | tf_op jit(solution)/shard_map/ppermute | solution.py:106
  22.3 8.7 %collective-permute-done.1 = bf16[256,512]{1,0:T(8,128)(2,1)S(1)} collective-permute-done((bf16[256,512]{1,0:T(8,128)(2,1)S(1)}, bf16[256,512]{1,0:T(8,128)(2,1)S(1)}, u32[]{:S(2)}, u32[]{:S(2)}) %collective-permute-start.1) | collective-permute-done | bytes 262176 | tf_op jit(solution)/shard_map/ppermute | solution.py:106
  31.0 7.9 %collective-permute-done.2 = bf16[256,512]{1,0:T(8,128)(2,1)S(1)} collective-permute-done((bf16[256,512]{1,0:T(8,128)(2,1)S(1)}, bf16[256,512]{1,0:T(8,128)(2,1)S(1)}, u32[]{:S(2)}, u32[]{:S(2)}) %collective-permute-start.2) | collective-permute-done | bytes 262176 | tf_op jit(solution)/shard_map/ppermute | solution.py:106
  40.2 6.3 %collective-permute-done.3 = bf16[256,512]{1,0:T(8,128)(2,1)S(1)} collective-permute-done((bf16[256,512]{1,0:T(8,128)(2,1)S(1)}, bf16[256,512]{1,0:T(8,128)(2,1)S(1)}, u32[]{:S(2)}, u32[]{:S(2)}) %collective-permute-start.3) | collective-permute-done | bytes 262176 | tf_op jit(solution)/shard_map/ppermute | solution.py:106
  46.7 8.3 %collective-permute-done.4 = bf16[256,512]{1,0:T(8,128)(2,1)S(1)} collective-permute-done((bf16[256,512]{1,0:T(8,128)(2,1)S(1)}, bf16[256,512]{1,0:T(8,128)(2,1)S(1)}, u32[]{:S(2)}, u32[]{:S(2)}) %collective-permute-start.4) | collective-permute-done | bytes 262176 | tf_op jit(solution)/shard_map/ppermute | solution.py:106
  55.2 9.4 %collective-permute-done.5 = bf16[256,512]{1,0:T(8,128)(2,1)S(1)} collective-permute-done((bf16[256,512]{1,0:T(8,128)(2,1)S(1)}, bf16[256,512]{1,0:T(8,128)(2,1)S(1)}, u32[]{:S(2)}, u32[]{:S(2)}) %collective-permute-start.5) | collective-permute-done | bytes 262176 | tf_op jit(solution)/shard_map/ppermute | solution.py:106
  64.7 7.5 %collective-permute-done.6 = bf16[256,512]{1,0:T(8,128)(2,1)S(1)} collective-permute-done((bf16[256,512]{1,0:T(8,128)(2,1)S(1)}, bf16[256,512]{1,0:T(8,128)(2,1)S(1)}, u32[]{:S(2)}, u32[]{:S(2)}) %collective-permute-start.6) | collective-permute-done | bytes 262176 | tf_op jit(solution)/shard_map/ppermute | solution.py:106
  84.3 4.1 fusion.1
  91.4 20.9 %all-gather.2 = bf16[32,1,8]{2,1,0:T(2,128)(2,1)S(1)} all-gather(bf16[1,1,8]{2,1,0:T(2,128)(2,1)S(1)} %bitcast.151), channel_id=1, replica_groups=mesh['seq'=32,'tp'=8] {'seq'}, dimensions={0}, use_global_device_ids=true | all-gather | bytes 528 | tf_op jit(solution)/shard_map/all_gather | solution.py:19
  115.3 26.1 %all-gather.15.cloned.1.call-done = bf16[256,128,64]{1,2,0:T(8,128)(2,1)} async-done(((bf16[8,128,64]{1,2,0:T(8,128)(2,1)}), bf16[256,128,64]{1,2,0:T(8,128)(2,1)}) %all-gather.15.cloned.1.call-update) | async-done | bytes 4194320 | tf_op jit(solution)/shard_map/all_gather | solution.py:19
  141.5 32.8 %while.16 = (s32[]{:T(128)}, f32[8,128,64]{2,1,0:T(8,128)S(1)}, s32[]{:T(128)}, bf16[32,8,128,64]{2,3,1,0:T(8,128)(2,1)}, bf16[32,8]{1,0:T(8,128)(2,1)S(1)}, /*index=5*/s32[]{:T(128)}, s32[]{:T(128)}, s32[]{:T(128)}, s32[]{:T(128)}) while((s32[]{:T(128)}, f32[8,128,64]{2,1,0:T(8,128)S(1)}, s32[]{:T(128)}, bf16[32,8,128,64]{2,3,1,0:T(8,128)(2,1)}, ...), condition=%wide.region_5.6_spmd, body=%wide.region_4.5_spmd.sunk | while | flops 196622 | bytes 1179883 | solution.py:34
  175.3 8.8 %all-gather.13.cloned.1.call-done = bf16[256,4096]{1,0:T(8,128)(2,1)} async-done(((bf16[256,512]{1,0:T(8,128)(2,1)}), bf16[256,4096]{1,0:T(8,128)(2,1)}) %all-gather.13.cloned.1.call-update) | async-done | bytes 2097168 | tf_op jit(solution)/shard_map/all_gather | solution.py:103
  184.2 4.8 fusion
  189.0 6.5 %copy.85 = bf16[4096,512]{1,0:T(8,128)(2,1)} copy(bf16[4096,512]{0,1:T(8,128)(2,1)} %fusion) | data formatting | bytes 8388608
  196.5 87.0 %reduce-scatter.10.cloned.1.call-done = bf16[128,512]{1,0:T(8,128)(2,1)} async-done(((bf16[4096,512]{1,0:T(8,128)(2,1)}), bf16[128,512]{1,0:T(8,128)(2,1)}) %reduce-scatter.10.cloned.1.call-update) | async-done | bytes 131088
  285.4 54.8 %all-gather.11.cloned.1.call-done = bf16[4096,512]{0,1:T(8,128)(2,1)} async-done(((bf16[128,512]{0,1:T(8,128)(2,1)}), bf16[4096,512]{0,1:T(8,128)(2,1)}) %all-gather.11.cloned.1.call-update) | async-done | bytes 4194320 | tf_op jit(solution)/shard_map/all_gather | solution.py:101
  349.1 47.4 %all-gather.17.cloned.1.call-done = bf16[256,128,64]{1,2,0:T(8,128)(2,1)} async-done(((bf16[8,128,64]{1,2,0:T(8,128)(2,1)}), bf16[256,128,64]{1,2,0:T(8,128)(2,1)}) %all-gather.17.cloned.1.call-update) | async-done | bytes 4194320 | tf_op jit(solution)/shard_map/all_gather | solution.py:19
  396.6 7.8 %while.17 = (s32[]{:T(128)}, f32[8,128,64]{2,1,0:T(8,128)S(1)}, s32[]{:T(128)}, bf16[32,8]{1,0:T(8,128)(2,1)S(1)}, bf16[32,8,128,64]{2,3,1,0:T(8,128)(2,1)}, /*index=5*/s32[]{:T(128)}, s32[]{:T(128)}, s32[]{:T(128)}) while((s32[]{:T(128)}, f32[8,128,64]{2,1,0:T(8,128)S(1)}, s32[]{:T(128)}, bf16[32,8]{1,0:T(8,128)(2,1)S(1)}, ...), condition=%wide.region_11.12_spmd, body=%wide.region_10.11_spmd.sunk | while | flops 196621 | bytes 1179863 | solution.py:34
  405.4 4.9 convolution_convert_fusion
  410.5 4.9 convolution_convert_fusion.2
  416.3 83.4 %psum.14 = f32[512]{0:T(512)S(1)} all-reduce(f32[512]{0:T(512)S(1)} %get-tuple-element.273), channel_id=1, replica_groups=mesh['seq'=32,'tp'=8] {'seq'}, use_global_device_ids=true, to_apply=%region_9.10 | all-reduce | flops 512 | bytes 4096 | tf_op jit(solution)/shard_map/psum | solution.py:174
  500.2 30.9 %reduce-scatter.12.cloned.1.call-done = bf16[128,512]{1,0:T(8,128)(2,1)} async-done(((bf16[4096,512]{1,0:T(8,128)(2,1)}), bf16[128,512]{1,0:T(8,128)(2,1)}) %reduce-scatter.12.cloned.1.call-update) | async-done | bytes 131088
  533.2 17.5 %psum.15 = f32[128]{0:T(128)S(1)} all-reduce(f32[128]{0:T(128)S(1)} %get-tuple-element.275), channel_id=1, replica_groups=mesh['seq'=32,'tp'=8] {'tp'}, use_global_device_ids=true, to_apply=%region_14.15 | all-reduce | flops 128 | bytes 1024 | tf_op jit(solution)/shard_map/psum | solution.py:175
  551.2 25.1 %reduce-scatter.8.cloned.1.call-done = bf16[256,512]{1,0:T(8,128)(2,1)} async-done(((bf16[256,4096]{1,0:T(8,128)(2,1)}), bf16[256,512]{1,0:T(8,128)(2,1)}) %reduce-scatter.8.cloned.1.call-update) | async-done | bytes 262160 | tf_op jit(solution)/shard_map/reduce_scatter | solution.py:169
  (231 shorter events, 81.7 us)
Async XLA Ops:
  7.2 105.4 %copy-start = (bf16[256,128]{1,0:T(8,128)(2,1)S(1)}, bf16[256,128]{1,0:T(8,128)(2,1)}, u32[]{:S(2)}) copy-start(bf16[256,128]{1,0:T(8,128)(2,1)} %param.19) | copy-start | bytes 196612
  7.2 70.3 %copy-start.2 = (bf16[256,512]{1,0:T(8,128)(2,1)S(1)}, bf16[256,512]{1,0:T(8,128)(2,1)}, u32[]{:S(2)}) copy-start(bf16[256,512]{1,0:T(8,128)(2,1)} %param.14) | copy-start | bytes 786436
  7.2 77.1 %all-gather.9.cloned.1.call-start = ((), (), s32[]{:S(2)}) async-start(), calls=%async_computation.3 | async-start | bytes 4325376 | tf_op jit(solution)/shard_map/all_gather | solution.py:102
  9.8 131.6 %all-gather.15.cloned.1.call-start = ((), (), s32[]{:S(2)}) async-start(), calls=%async_computation.7 | async-start | bytes 4325376 | tf_op jit(solution)/shard_map/all_gather | solution.py:19
  9.9 12.5 %collective-permute-start = (bf16[256,512]{1,0:T(8,128)(2,1)}, bf16[256,512]{1,0:T(8,128)(2,1)S(1)}, u32[]{:S(2)}, u32[]{:S(2)}) collective-permute-start(bf16[256,512]{1,0:T(8,128)(2,1)} %param.14), channel_id=1, source_target_pairs={{0,1},{1,2},{2,3},{3,4},{4,5},{5,6},{6,7},{7,0},{8,9},{9,10},{10,1... | collective-permute-start | bytes 786440 | tf_op jit(solution)/shard_map/ppermute | solution.py:106
  22.3 8.7 %collective-permute-start.1 = (bf16[256,512]{1,0:T(8,128)(2,1)S(1)}, bf16[256,512]{1,0:T(8,128)(2,1)S(1)}, u32[]{:S(2)}, u32[]{:S(2)}) collective-permute-start(bf16[256,512]{1,0:T(8,128)(2,1)S(1)} %collective-permute-done), channel_id=1, source_target_pairs={{0,1},{1,2},{2,3},{3,4},{4,5},{5,6},{6,7},{7,0},{8,9},{9,10},{10,1... | collective-permute-start | bytes 786440 | tf_op jit(solution)/shard_map/ppermute | solution.py:106
  31.0 7.9 %collective-permute-start.2 = (bf16[256,512]{1,0:T(8,128)(2,1)S(1)}, bf16[256,512]{1,0:T(8,128)(2,1)S(1)}, u32[]{:S(2)}, u32[]{:S(2)}) collective-permute-start(bf16[256,512]{1,0:T(8,128)(2,1)S(1)} %collective-permute-done.1), channel_id=1, source_target_pairs={{0,1},{1,2},{2,3},{3,4},{4,5},{5,6},{6,7},{7,0},{8,9},{9,10},{10,1... | collective-permute-start | bytes 786440 | tf_op jit(solution)/shard_map/ppermute | solution.py:106
  38.9 7.6 %collective-permute-start.3 = (bf16[256,512]{1,0:T(8,128)(2,1)S(1)}, bf16[256,512]{1,0:T(8,128)(2,1)S(1)}, u32[]{:S(2)}, u32[]{:S(2)}) collective-permute-start(bf16[256,512]{1,0:T(8,128)(2,1)S(1)} %collective-permute-done.2), channel_id=1, source_target_pairs={{0,1},{1,2},{2,3},{3,4},{4,5},{5,6},{6,7},{7,0},{8,9},{9,10},{10,1... | collective-permute-start | bytes 786440 | tf_op jit(solution)/shard_map/ppermute | solution.py:106
  46.5 8.5 %collective-permute-start.4 = (bf16[256,512]{1,0:T(8,128)(2,1)S(1)}, bf16[256,512]{1,0:T(8,128)(2,1)S(1)}, u32[]{:S(2)}, u32[]{:S(2)}) collective-permute-start(bf16[256,512]{1,0:T(8,128)(2,1)S(1)} %collective-permute-done.3), channel_id=1, source_target_pairs={{0,1},{1,2},{2,3},{3,4},{4,5},{5,6},{6,7},{7,0},{8,9},{9,10},{10,1... | collective-permute-start | bytes 786440 | tf_op jit(solution)/shard_map/ppermute | solution.py:106
  55.0 9.6 %collective-permute-start.5 = (bf16[256,512]{1,0:T(8,128)(2,1)S(1)}, bf16[256,512]{1,0:T(8,128)(2,1)S(1)}, u32[]{:S(2)}, u32[]{:S(2)}) collective-permute-start(bf16[256,512]{1,0:T(8,128)(2,1)S(1)} %collective-permute-done.4), channel_id=1, source_target_pairs={{0,1},{1,2},{2,3},{3,4},{4,5},{5,6},{6,7},{7,0},{8,9},{9,10},{10,1... | collective-permute-start | bytes 786440 | tf_op jit(solution)/shard_map/ppermute | solution.py:106
  64.6 7.6 %collective-permute-start.6 = (bf16[256,512]{1,0:T(8,128)(2,1)S(1)}, bf16[256,512]{1,0:T(8,128)(2,1)S(1)}, u32[]{:S(2)}, u32[]{:S(2)}) collective-permute-start(bf16[256,512]{1,0:T(8,128)(2,1)S(1)} %collective-permute-done.5), channel_id=1, source_target_pairs={{0,1},{1,2},{2,3},{3,4},{4,5},{5,6},{6,7},{7,0},{8,9},{9,10},{10,1... | collective-permute-start | bytes 786440 | tf_op jit(solution)/shard_map/ppermute | solution.py:106
  64.7 19.6 %copy-start.10 = (f32[4096]{0:T(1024)S(1)}, f32[4096]{0:T(1024)}, u32[]{:S(2)}) copy-start(f32[4096]{0:T(1024)} %param.18) | copy-start | bytes 49156
  84.3 4.2 copy-start.3
  84.3 6.0 %copy-start.8 = (f32[256,8]{0,1:T(8,128)S(1)}, f32[256,8]{0,1:T(8,128)}, u32[]{:S(2)}) copy-start(f32[256,8]{0,1:T(8,128)} %param.21) | copy-start | bytes 24580
  89.5 94.7 %all-gather.13.cloned.1.call-start = ((), (), s32[]{:S(2)}) async-start(), calls=%async_computation.6 | async-start | bytes 2359296 | tf_op jit(solution)/shard_map/all_gather | solution.py:103
  90.3 193.2 %reduce-scatter.10.cloned.1.call-start = ((), (), s32[]{:S(2)}) async-start(), calls=%async_computation.9 | async-start | bytes 4325376
  195.5 0.9 copy-start.7
  195.5 89.0 %copy-start.9 = (f32[512]{0:T(512)S(1)}, f32[512]{0:T(512)}, u32[]{:S(2)}) copy-start(f32[512]{0:T(512)} %param.16) | copy-start | bytes 6148
  195.5 144.7 %copy-start.1 = (bf16[256,4096]{1,0:T(8,128)(2,1)S(1)}, bf16[256,4096]{1,0:T(8,128)(2,1)}, u32[]{:S(2)}) copy-start(bf16[256,4096]{1,0:T(8,128)(2,1)} %all-gather.13.cloned.1.call-done) | copy-start | bytes 6291460
  195.5 144.7 %all-gather.11.cloned.1.call-start = ((), (), s32[]{:S(2)}) async-start(), calls=%async_computation.4 | async-start | bytes 4325376 | tf_op jit(solution)/shard_map/all_gather | solution.py:101
  285.4 60.3 %copy-start.6 = (f32[256,256]{1,0:T(8,128)S(1)}, f32[256,256]{1,0:T(8,128)}, u32[]{:S(2)}) copy-start(f32[256,256]{1,0:T(8,128)} %copy-done.5) | copy-start | bytes 786436
  285.4 111.2 %all-gather.17.cloned.1.call-start = ((), (), s32[]{:S(2)}) async-start(), calls=%async_computation.8 | async-start | bytes 4325376 | tf_op jit(solution)/shard_map/all_gather | solution.py:19
  345.6 185.6 %reduce-scatter.12.cloned.1.call-start = ((), (), s32[]{:S(2)}) async-start(), calls=%async_computation.10 | async-start | bytes 4325376
  410.3 166.0 %reduce-scatter.8.cloned.1.call-start = ((), (), s32[]{:S(2)}) async-start(), calls=%async_computation.5 | async-start | bytes 2359296 | tf_op jit(solution)/shard_map/reduce_scatter | solution.py:169
  (2 other events, 1.5 us)
Sparse Core Ops, SparseCore 0:
  11.1 56.6 all-gather.8
  89.6 51.7 all-gather.14
  143.2 40.8 all-gather.12
  195.6 87.7 reduce-scatter.9
  286.6 53.5 all-gather.10
  345.7 50.7 all-gather.16
  410.5 120.6 reduce-scatter.11
  534.3 41.9 reduce-scatter.7
